TPU v7x, 32 devices: a whole 2x2x4 slice. The times are simulated.
32 devices in a mesh: dp: 8 (over z, x), tok: 4 (over y, core).
Axes of the slice: x: 2, y: 2, z: 4, core: 2. Of those that a mesh axis runs over, the one named last changes fastest.
Arguments:
- inputs: bfloat16 [128, 200, 384], P(('dp', 'tok')), may hold values from -6 to 6
- cotangent: bfloat16 [128, 200, 384], P(('dp', 'tok')), may hold values from -6 to 6
- lengths: int32 [128], P('dp'), may hold values from 1 to 198, 12672 in all
- w_qkv: float32 [2, 384, 1152], P(None, None, 'dp'), may hold values from -0.3125 to 0.3125
- w_proj: float32 [2, 384, 384], P(None, None, 'dp'), may hold values from -0.875 to 0.875
- w_fc1: float32 [2, 384, 1536], P(None, None, 'dp'), may hold values from -0.3125 to 0.3125
- w_fc2: float32 [2, 1536, 384], P(None, 'dp'), may hold values from -0.15625 to 0.15625
- norm_gains: float32 [2, 2, 384], P(None, None, 'dp'), may hold values from 0.5 to 1.5
- biases: float32 [2, 3840], P(None, 'dp'), may hold values from -1.75 to 1.75
- mom_qkv: float32 [2, 2, 384, 1152], P(None, None, None, 'dp'), as said below
- mom_proj: float32 [2, 2, 384, 384], P(None, None, None, 'dp'), as said below
- mom_fc1: float32 [2, 2, 384, 1536], P(None, None, None, 'dp'), as said below
- mom_fc2: float32 [2, 2, 1536, 384], P(None, None, 'dp'), as said below
- mom_gains: float32 [2, 2, 2, 384], P(None, None, None, 'dp'), as said below
- mom_biases: float32 [2, 2, 3840], P(None, None, 'dp'), as said below
Outputs:
- layer_out: bfloat16 [128, 200, 384], P(('dp', 'tok'))
- input_grad: float32 [128, 200, 384], P(('dp', 'tok'))
- grad_norm: float32 [], replicated
- state_qkv: float32 [2, 2, 384, 1152], P(None, None, None, 'dp')
- state_proj: float32 [2, 2, 384, 384], P(None, None, None, 'dp')
- state_fc1: float32 [2, 2, 384, 1536], P(None, None, None, 'dp')
- state_fc2: float32 [2, 2, 1536, 384], P(None, None, 'dp')
- state_gains: float32 [2, 2, 2, 384], P(None, None, None, 'dp')
- state_biases: float32 [2, 2, 3840], P(None, None, 'dp')
- second_moments: float32 [3548160], P('dp')
Inputs may be any that keep to these rules, and one draw needn't show every extreme that they name: Sequence i keeps its first lengths[i] slots; some sequence keeps all 198. `mom_qkv`: index 0 holds the first moment, index 1 the second moment, which is positive. `mom_proj`: index 0 holds the first moment, index 1 the second moment, which is positive. `mom_fc1`: index 0 holds the first moment, index 1 the second moment, which is positive. `mom_fc2`: index 0 holds the first moment, index 1 the second moment, which is positive. `mom_gains`: index 0 holds the first moment, index 1 the second moment, which is positive. `mom_biases`: index 0 holds the first moment, index 1 the second moment, which is positive.
All inputs are finite; a program needn't handle non-finite values. No bound on the sum of `lengths` on one device may be relied on, other than what follows from the above.
Results may differ from a plain program's by a relative error of at most 0.018.
The roundings to bfloat16 on the way count: a program that leaves them out, or rounds other values in their place, can miss the bound.
Values may be sent and summed in bfloat16 or wider, within the bound.
No kernel may reach another device: no remote copies, remote signals or barrier semaphores. Data moves between devices by JAX's collectives and lax.ppermute only.
A program may use at most 128 MiB of HBM per device.

v0:
```python
import math
import jax
import jax.numpy as jnp
from jax import lax
from jax.sharding import PartitionSpec as P

D = 384
HEADS = 6
HD = 64
FF = 1536
LAYERS = 2
STEP = 10
HALF_ROOT = 0.7071067811865476
INV_ROOT_TAU = 0.3989422804014327


def normalize(hidden):
    row_mean = jnp.mean(hidden, -1, keepdims=True)
    centered = hidden - row_mean
    variance = jnp.mean(centered * centered, -1, keepdims=True)
    inverse = lax.rsqrt(variance + 1e-06)
    return (centered * inverse, inverse)


def norm_back(grad_n, normed, inverse):
    first_mean = jnp.mean(grad_n, -1, keepdims=True)
    second_mean = jnp.mean(grad_n * normed, -1, keepdims=True)
    return inverse * (grad_n - first_mean - normed * second_mean)


def gelu_slope(pre_act):
    return (
        0.5 * (1.0 + lax.erf(pre_act * HALF_ROOT))
        + pre_act * jnp.exp(-0.5 * pre_act * pre_act) * INV_ROOT_TAU
    )


def spread_heads(tensor, axis):
    first = lax.slice_in_dim(tensor, 0, 5, axis=axis)
    last = lax.slice_in_dim(tensor, 5, 6, axis=axis)
    empty = jnp.zeros_like(last)
    return jnp.concatenate([first, empty, last, empty], axis)


def pick_heads(tensor, axis):
    first = lax.slice_in_dim(tensor, 0, 5, axis=axis)
    last = lax.slice_in_dim(tensor, 6, 7, axis=axis)
    return jnp.concatenate([first, last], axis)


def qkv_to_heads(packed):
    seq_count, slot_total = (packed.shape[0], packed.shape[1])
    sending = spread_heads(packed, 3).reshape(seq_count, slot_total, 3, 4, 2 * HD)
    arrived = lax.all_to_all(sending, "tok", split_axis=3, concat_axis=0, tiled=True)
    return arrived.reshape(4 * seq_count, slot_total, 3, 2, HD)


def out_to_rows(attended):
    batch_size, slot_total = (attended.shape[0], attended.shape[1])
    sending = attended.reshape(batch_size, slot_total, 1, 2 * HD)
    arrived = lax.all_to_all(sending, "tok", split_axis=0, concat_axis=2, tiled=True)
    return pick_heads(arrived.reshape(batch_size // 4, slot_total, 8, HD), 2)


def dout_to_heads(grad_rows):
    seq_count, slot_total = (grad_rows.shape[0], grad_rows.shape[1])
    sending = spread_heads(grad_rows, 2).reshape(seq_count, slot_total, 4, 2 * HD)
    arrived = lax.all_to_all(sending, "tok", split_axis=2, concat_axis=0, tiled=True)
    return arrived.reshape(4 * seq_count, slot_total, 2, HD)


def grads_to_rows(stacked):
    batch_size, slot_total = (stacked.shape[0], stacked.shape[1])
    sending = stacked.reshape(batch_size, slot_total, 3, 1, 2 * HD)
    arrived = lax.all_to_all(sending, "tok", split_axis=0, concat_axis=3, tiled=True)
    return pick_heads(arrived.reshape(batch_size // 4, slot_total, 3, 8, HD), 3)


def score_block(query_b, key_b, lens_block):
    scores = (
        jnp.einsum("bqhd,bkhd->bhqk", query_b, key_b, preferred_element_type=jnp.float32) * 0.125
    )
    key_mask = jnp.arange(key_b.shape[1])[None, :] < lens_block[:, None]
    return jnp.where(key_mask[:, None, None, :], scores, -1e30)


def forward_block(packed):
    stacked, lens_block = packed
    query_b = stacked[:, :, 0]
    key_b = stacked[:, :, 1]
    value_b = stacked[:, :, 2]
    scores = score_block(query_b, key_b, lens_block)
    row_max = jnp.max(scores, -1, keepdims=True)
    exp_part = jnp.exp(scores - row_max)
    summed = jnp.sum(exp_part, -1, keepdims=True)
    prob_low = (exp_part / summed).astype(jnp.bfloat16)
    result = jnp.einsum("bhqk,bkhd->bqhd", prob_low, value_b, preferred_element_type=jnp.float32)
    return (result.astype(jnp.bfloat16), (row_max + jnp.log(summed))[..., 0])


def backward_block(packed):
    stacked, lse_block, dout_block, lens_block = packed
    query_b = stacked[:, :, 0]
    key_b = stacked[:, :, 1]
    value_b = stacked[:, :, 2]
    scores = score_block(query_b, key_b, lens_block)
    prob_full = jnp.exp(scores - lse_block[..., None])
    grad_v = jnp.einsum(
        "bhqk,bqhd->bkhd",
        prob_full.astype(jnp.bfloat16),
        dout_block,
        preferred_element_type=jnp.float32,
    )
    grad_p = jnp.einsum("bqhd,bkhd->bhqk", dout_block, value_b, preferred_element_type=jnp.float32)
    inner_sum = jnp.sum(prob_full * grad_p, -1, keepdims=True)
    grad_s = (prob_full * (grad_p - inner_sum)).astype(jnp.bfloat16)
    grad_q = (
        jnp.einsum("bhqk,bkhd->bqhd", grad_s, key_b, preferred_element_type=jnp.float32) * 0.125
    )
    grad_k = (
        jnp.einsum("bhqk,bqhd->bkhd", grad_s, query_b, preferred_element_type=jnp.float32) * 0.125
    )
    return jnp.stack([grad_q, grad_k, grad_v], 2).astype(jnp.bfloat16)


def run_blocks(block_fn, arrays):
    batch_size = arrays[0].shape[0]
    folded = tuple((entry.reshape((batch_size // 4, 4) + entry.shape[1:]) for entry in arrays))
    result = lax.map(block_fn, folded)

    def unfold(folded_part):
        return folded_part.reshape((batch_size,) + folded_part.shape[2:])

    return jax.tree.map(unfold, result)


def sum_squares(tensors):
    return sum((jnp.sum(entry * entry) for entry in tensors))


def adamw(weight, moments, clipped, rate, decay):
    first_mom = 0.9 * moments[0] + 0.1 * clipped
    second_mom = 0.999 * moments[1] + 0.001 * clipped * clipped
    fixed_first = first_mom / (1.0 - 0.9**STEP)
    fixed_second = second_mom / (1.0 - 0.999**STEP)
    new_weight = weight - rate * (fixed_first / (jnp.sqrt(fixed_second) + 1e-08) + decay * weight)
    return (jnp.stack([new_weight, first_mom]), second_mom)


def on_device(
    inputs,
    cotangent,
    lengths,
    w_qkv,
    w_proj,
    w_fc1,
    w_fc2,
    norm_gains,
    biases,
    mom_qkv,
    mom_proj,
    mom_fc1,
    mom_fc2,
    mom_gains,
    mom_biases,
):
    full_qkv, full_proj, full_fc1, full_fc2, full_gains, full_biases = (
        lax.all_gather(w_qkv.astype(jnp.bfloat16), "dp", axis=2, tiled=True),
        lax.all_gather(w_proj.astype(jnp.bfloat16), "dp", axis=2, tiled=True),
        lax.all_gather(w_fc1.astype(jnp.bfloat16), "dp", axis=2, tiled=True),
        lax.all_gather(w_fc2.astype(jnp.bfloat16), "dp", axis=1, tiled=True),
        lax.all_gather(norm_gains.astype(jnp.bfloat16), "dp", axis=2, tiled=True),
        lax.all_gather(biases.astype(jnp.bfloat16), "dp", axis=1, tiled=True),
    )
    seq_count = inputs.shape[0]
    slot_total = inputs.shape[1]
    row_count = seq_count * slot_total
    tok_index = lax.axis_index("tok")
    own_lengths = lax.dynamic_slice_in_dim(lengths, tok_index * seq_count, seq_count, 0)
    positions = jnp.arange(slot_total)
    valid = (positions[None, :] < own_lengths[:, None]).reshape(row_count, 1)
    hidden = inputs.astype(jnp.float32).reshape(row_count, D)
    saved = []
    for layer_id in range(LAYERS):
        q_weight = full_qkv[layer_id]
        o_weight = full_proj[layer_id]
        up_weight = full_fc1[layer_id]
        down_weight = full_fc2[layer_id]
        gain_rows = full_gains[layer_id].astype(jnp.float32)
        bias_row = full_biases[layer_id].astype(jnp.float32)
        norm_first, inv_first = normalize(hidden)
        a_first = (norm_first * gain_rows[0] + bias_row[0:D]).astype(jnp.bfloat16)
        qkv_bias = jnp.concatenate(
            [bias_row[D : 2 * D], jnp.zeros((D,), jnp.float32), bias_row[2 * D : 3 * D]]
        )
        qkv = jnp.dot(a_first, q_weight, preferred_element_type=jnp.float32) + qkv_bias
        qkv = qkv.astype(jnp.bfloat16).reshape(seq_count, slot_total, 3, HEADS, HD)
        head_qkv = qkv_to_heads(qkv)
        attended, lse_all = run_blocks(forward_block, (head_qkv, lengths))
        att_rows = out_to_rows(attended).reshape(row_count, D)
        mid_hidden = (
            hidden
            + jnp.dot(att_rows, o_weight, preferred_element_type=jnp.float32)
            + bias_row[3 * D : 4 * D]
        )
        norm_second, inv_second = normalize(mid_hidden)
        a_second = (norm_second * gain_rows[1] + bias_row[4 * D : 5 * D]).astype(jnp.bfloat16)
        pre_act = (
            jnp.dot(a_second, up_weight, preferred_element_type=jnp.float32) + bias_row[6 * D :]
        )
        activated = jax.nn.gelu(pre_act, approximate=False).astype(jnp.bfloat16)
        hidden = (
            mid_hidden
            + jnp.dot(activated, down_weight, preferred_element_type=jnp.float32)
            + bias_row[5 * D : 6 * D]
        )
        saved.append(
            (
                norm_first,
                inv_first,
                a_first,
                head_qkv,
                lse_all,
                att_rows,
                norm_second,
                inv_second,
                a_second,
                pre_act,
                activated,
            )
        )
    layer_out = jnp.where(valid, hidden, 0.0).astype(jnp.bfloat16).reshape(inputs.shape)
    grad_h = cotangent.astype(jnp.float32).reshape(row_count, D) * valid.astype(jnp.float32)
    list_qkv = [None] * LAYERS
    list_proj = [None] * LAYERS
    list_fc1 = [None] * LAYERS
    list_fc2 = [None] * LAYERS
    list_gains = [None] * LAYERS
    list_biases = [None] * LAYERS
    for layer_id in range(LAYERS - 1, -1, -1):
        (
            norm_first,
            inv_first,
            a_first,
            head_qkv,
            lse_all,
            att_rows,
            norm_second,
            inv_second,
            a_second,
            pre_act,
            activated,
        ) = saved[layer_id]
        q_weight = full_qkv[layer_id]
        o_weight = full_proj[layer_id]
        up_weight = full_fc1[layer_id]
        down_weight = full_fc2[layer_id]
        gain_rows = full_gains[layer_id].astype(jnp.float32)
        grad_m = grad_h.astype(jnp.bfloat16)
        list_fc2[layer_id] = jnp.einsum(
            "rf,rd->fd", activated, grad_m, preferred_element_type=jnp.float32
        )
        bias_fc2 = jnp.sum(grad_m, 0, dtype=jnp.float32)
        grad_act = jnp.einsum("rd,fd->rf", grad_m, down_weight, preferred_element_type=jnp.float32)
        grad_up = (grad_act * gelu_slope(pre_act)).astype(jnp.bfloat16)
        list_fc1[layer_id] = jnp.einsum(
            "rd,rf->df", a_second, grad_up, preferred_element_type=jnp.float32
        )
        bias_fc1 = jnp.sum(grad_up, 0, dtype=jnp.float32)
        grad_a2 = jnp.einsum("rf,df->rd", grad_up, up_weight, preferred_element_type=jnp.float32)
        gain_second = jnp.sum(grad_a2 * norm_second, 0)
        bias_ln2 = jnp.sum(grad_a2, 0)
        grad_mid = grad_h + norm_back(grad_a2 * gain_rows[1], norm_second, inv_second)
        grad_p = grad_mid.astype(jnp.bfloat16)
        list_proj[layer_id] = jnp.einsum(
            "rd,re->de", att_rows, grad_p, preferred_element_type=jnp.float32
        )
        bias_proj = jnp.sum(grad_p, 0, dtype=jnp.float32)
        grad_att = jnp.einsum("re,de->rd", grad_p, o_weight, preferred_element_type=jnp.float32)
        grad_att = grad_att.astype(jnp.bfloat16).reshape(seq_count, slot_total, HEADS, HD)
        head_dout = dout_to_heads(grad_att)
        head_grads = run_blocks(backward_block, (head_qkv, lse_all, head_dout, lengths))
        grad_qkv = grads_to_rows(head_grads).reshape(row_count, 3 * D)
        list_qkv[layer_id] = jnp.einsum(
            "rd,rc->dc", a_first, grad_qkv, preferred_element_type=jnp.float32
        )
        bias_q = jnp.sum(grad_qkv[:, 0:D], 0, dtype=jnp.float32)
        bias_v = jnp.sum(grad_qkv[:, 2 * D : 3 * D], 0, dtype=jnp.float32)
        grad_a1 = jnp.einsum("rc,dc->rd", grad_qkv, q_weight, preferred_element_type=jnp.float32)
        gain_first = jnp.sum(grad_a1 * norm_first, 0)
        bias_ln1 = jnp.sum(grad_a1, 0)
        grad_h = grad_mid + norm_back(grad_a1 * gain_rows[0], norm_first, inv_first)
        list_gains[layer_id] = jnp.stack([gain_first, gain_second])
        list_biases[layer_id] = jnp.concatenate(
            [bias_ln1, bias_q, bias_v, bias_proj, bias_ln2, bias_fc2, bias_fc1]
        )
    input_grad = grad_h.reshape(inputs.shape)
    grad_qkv_all = jnp.stack(list_qkv)
    grad_proj_all = jnp.stack(list_proj)
    grad_fc1_all = jnp.stack(list_fc1)
    grad_fc2_all = jnp.stack(list_fc2)
    grad_gain_all = jnp.stack(list_gains)
    grad_bias_all = jnp.stack(list_biases)
    masters = (w_qkv, w_proj, w_fc1, w_fc2, norm_gains, biases)
    shard_dims = (2, 2, 2, 1, 2, 1)
    dp_index = lax.axis_index("dp")
    summed = lax.psum(
        (grad_qkv_all, grad_proj_all, grad_fc1_all, grad_fc2_all, grad_gain_all, grad_bias_all),
        ("dp", "tok"),
    )
    squares = sum_squares(summed)
    shares = tuple(
        (
            lax.dynamic_slice_in_dim(
                summed_part, dp_index * owner.shape[shard_dim], owner.shape[shard_dim], shard_dim
            )
            for summed_part, owner, shard_dim in zip(summed, masters, shard_dims)
        )
    )
    grad_norm = jnp.sqrt(squares)
    limit = 0.25 * math.sqrt(LAYERS * (4 * D * D + 2 * D * FF + 8 * D + FF))
    factor = jnp.minimum(1.0, limit / (grad_norm + 1e-06))
    state_qkv, second_qkv = adamw(w_qkv, mom_qkv, shares[0] * factor, 0.08, 0.05)
    state_proj, second_proj = adamw(w_proj, mom_proj, shares[1] * factor, 0.08, 0.05)
    state_fc1, second_fc1 = adamw(w_fc1, mom_fc1, shares[2] * factor, 0.08, 0.05)
    state_fc2, second_fc2 = adamw(w_fc2, mom_fc2, shares[3] * factor, 0.08, 0.05)
    state_gains, second_gains = adamw(norm_gains, mom_gains, shares[4] * factor, 0.4, 0.0)
    state_biases, second_biases = adamw(biases, mom_biases, shares[5] * factor, 0.4, 0.0)
    second_moments = jnp.concatenate(
        [
            second_qkv.reshape(-1),
            second_proj.reshape(-1),
            second_fc1.reshape(-1),
            second_fc2.reshape(-1),
            second_gains.reshape(-1),
            second_biases.reshape(-1),
        ]
    )
    return (
        layer_out,
        input_grad,
        grad_norm,
        state_qkv,
        state_proj,
        state_fc1,
        state_fc2,
        state_gains,
        state_biases,
        second_moments,
    )


def solution(mesh):
    placed = (
        P(("dp", "tok"), None, None),
        P(("dp", "tok"), None, None),
        P("dp"),
        P(None, None, "dp"),
        P(None, None, "dp"),
        P(None, None, "dp"),
        P(None, "dp", None),
        P(None, None, "dp"),
        P(None, "dp"),
        P(None, None, None, "dp"),
        P(None, None, None, "dp"),
        P(None, None, None, "dp"),
        P(None, None, "dp", None),
        P(None, None, None, "dp"),
        P(None, None, "dp"),
    )
    return jax.shard_map(
        on_device,
        mesh=mesh,
        in_specs=placed,
        out_specs=(
            P(("dp", "tok"), None, None),
            P(("dp", "tok"), None, None),
            P(),
            P(None, None, None, "dp"),
            P(None, None, None, "dp"),
            P(None, None, None, "dp"),
            P(None, None, "dp", None),
            P(None, None, None, "dp"),
            P(None, None, "dp"),
            P("dp"),
        ),
        check_vma=False,
    )
```

profile of v0, /device:TPU:0, one launch (start us, length us, event | category | flops | bytes accessed | tf_op | source)
XLA Modules:
  0.0 898.1 jit_solution(4694405918327446632)
XLA Ops:
  9.7 27.9 %all-gather = bf16[8,480,2]{1,2,0:T(2,128)(2,1)S(1)} all-gather(bf16[1,480,2]{1,2,0:T(2,128)(2,1)S(1)} %convert_bitcast_fusion), channel_id=1, replica_groups=mesh['dp'=8,'tok'=4] {'dp'}, dimensions={0}, use_global_device_ids=true | all-gather | bytes 17280 | tf_op jit(solution)/shard_map/all_gather | solution.py:173
  38.5 31.1 %all_gather.18 = bf16[2,2,384]{1,0,2:T(2,128)(2,1)S(1)} all-gather(bf16[2,2,48]{1,0,2:T(2,128)(2,1)S(1)} %copy.330), channel_id=1, replica_groups=mesh['dp'=8,'tok'=4] {'dp'}, dimensions={2}, use_global_device_ids=true | all-gather | bytes 3456 | tf_op jit(solution)/shard_map/all_gather | solution.py:172
  73.5 4.9 slice_reduce_fusion
  83.9 5.7 reshape.586
  93.6 3.6 copy.334
  97.2 4.6 all-to-all-start
  103.4 28.1 %all-to-all-done = bf16[4,200,3,4,128]{4,1,2,0,3:T(8,128)(2,1)} async-done(((bf16[4,200,3,4,128]{4,1,2,0,3:T(8,128)(2,1)}), bf16[4,200,3,4,128]{4,1,2,0,3:T(8,128)(2,1)}, u32[]{:S(2)}, u32[]{:S(2)}) %all-to-all-start) | async-done | bytes 2457632 | tf_op jit(solution)/shard_map/all_to_all | solution.py:54
  136.3 13.3 %while.44 = (s32[]{:T(128)}, bf16[4,4,200,2,64]{2,4,3,1,0:T(8,128)(2,1)}, f32[4,4,2,200]{3,2,1,0:T(2,128)}, bf16[4,4,200,3,2,64]{2,5,4,1,3,0:T(8,128)(2,1)S(1)}, s32[4,4]{1,0:T(4,128)}, /*index=5*/s32[]{:T(128)}) while((s32[]{:T(128)}, bf16[4,4,200,2,64]{2,4,3,1,0:T(8,128)(2,1)}, f32[4,4,2,200]{3,2,1,0:T(2,128)}, ...), condition=%wide.region_5.6_spmd, body=%wide.region_2.5_spmd.sunk | while | flops 84581600 | bytes 6535325 | solution.py:129
  152.5 4.2 all-to-all-start.1
  160.9 33.1 %all_gather.21 = bf16[2,384,384]{1,2,0:T(8,128)(2,1)S(1)} all-gather(bf16[2,384,48]{1,2,0:T(8,128)(2,1)S(1)} %convert_element_type.200), channel_id=1, replica_groups=mesh['dp'=8,'tok'=4] {'dp'}, dimensions={2}, use_global_device_ids=true | all-gather | bytes 663552 | tf_op jit(solution)/shard_map/all_gather | solution.py:169
  198.3 14.6 %fusion.38 = (bf16[800,1536]{1,0:T(8,128)(2,1)}, f32[800,1536]{1,0:T(8,128)}) fusion(f32[1536]{0:T(1024)S(1)} %get-tuple-element.494, bf16[2,384,1536]{1,2,0:T(8,128)(2,1)} %all-gather.7.cloned.1.call-done, f32[800,384]{1,0:T(8,128)S(1)} %get-tuple-element.476, f32[384]{0:T(512)S(1)} %copy-done.70, f32[384]{0:T(512)S(1)} %copy-done.66, ...), kind=kOutput, calls=%fused_computation.94 | convolution fusion | flops 1026355200 | bytes 9796864 | tf_op jit(solution)/shard_map/dot_general | solution.py:209
  214.7 3.7 fusion.121
  223.2 5.7 reshape.591
  232.8 13.8 %copy.342 = bf16[4,200,3,4,128]{4,1,2,0,3:T(8,128)(2,1)} copy(bf16[4,200,3,4,128]{1,0,4,3,2:T(4,128)(2,1)S(1)} %bitcast.482) | data formatting | bytes 4915200 | tf_op jit(solution)/shard_map/reshape | solution.py:53
  246.6 4.6 all-to-all-start.2
  251.2 29.6 %all-to-all-done.2 = bf16[4,200,3,4,128]{4,1,2,0,3:T(8,128)(2,1)} async-done(((bf16[4,200,3,4,128]{4,1,2,0,3:T(8,128)(2,1)}), bf16[4,200,3,4,128]{4,1,2,0,3:T(8,128)(2,1)}, u32[]{:S(2)}, u32[]{:S(2)}) %all-to-all-start.2) | async-done | bytes 2457632 | tf_op jit(solution)/shard_map/all_to_all | solution.py:54
  285.0 8.3 while.45
  295.5 4.2 all-to-all-start.3
  302.7 9.1 %all-to-all-done.3 = bf16[16,200,1,128]{3,1,2,0:T(8,128)(2,1)} async-done(((bf16[16,200,1,128]{3,1,2,0:T(8,128)(2,1)}), bf16[16,200,1,128]{3,1,2,0:T(8,128)(2,1)}, u32[]{:S(2)}, u32[]{:S(2)}) %all-to-all-start.3) | async-done | bytes 819232 | tf_op jit(solution)/shard_map/all_to_all | solution.py:61
  323.4 12.8 %fusion.41 = (bf16[800,1536]{1,0:T(8,128)(2,1)}, f32[800,1536]{1,0:T(8,128)S(1)}) fusion(f32[1536]{0:T(1024)S(1)} %copy-done.85, bf16[2,384,1536]{1,2,0:T(8,128)(2,1)S(1)} %copy-done.111, f32[800,384]{1,0:T(8,128)S(1)} %get-tuple-element.482, f32[384]{0:T(512)S(1)} %copy-done.72, f32[384]{0:T(512)S(1)} %copy-done.65, f32[800]{0:T(1024)S(1)} %add_rsqrt_fusion, ...), kind=kOutput, calls=%fused_computation.97 | convolution fusion | flops 1026355200 | bytes 9801728 | tf_op jit(solution)/shard_map/dot_general | solution.py:209
  336.1 4.3 convert_reduce_fusion
  358.5 4.2 all-to-all-start.4
  362.7 12.1 %all-to-all-done.4 = bf16[4,200,4,128]{3,1,0,2:T(8,128)(2,1)} async-done(((bf16[4,200,4,128]{3,1,0,2:T(8,128)(2,1)}), bf16[4,200,4,128]{3,1,0,2:T(8,128)(2,1)}, u32[]{:S(2)}, u32[]{:S(2)}) %all-to-all-start.4) | async-done | bytes 819232 | tf_op jit(solution)/shard_map/all_to_all | solution.py:68
  379.1 23.6 %while.46 = (s32[]{:T(128)}, bf16[4,4,200,3,2,64]{2,5,4,3,1,0:T(8,128)(2,1)}, bf16[4,4,200,3,2,64]{2,5,4,1,3,0:T(8,128)(2,1)S(1)}, s32[4,4]{1,0:T(4,128)S(1)}, f...) while((s32[]{:T(128)}, bf16[4,4,200,3,2,64]{2,5,4,3,1,0:T(8,128)(2,1)}, ...), condition=%wide.region_20.21_spmd, body=%wide.region_18.20_spmd.sunk | while | flops 208805600 | bytes 15433129 | solution.py:129
  402.7 4.6 copy.354
  407.2 4.7 all-to-all-start.5
  411.9 4.7 convolution_bitcast_fusion.2
  416.6 24.9 %all-to-all-done.5 = bf16[16,200,3,1,128]{4,1,3,2,0:T(8,128)(2,1)} async-done(((bf16[16,200,3,1,128]{4,1,3,2,0:T(8,128)(2,1)}), bf16[16,200,3,1,128]{4,1,3,2,0:T(8,128)(2,1)}, u32[]{:S(2)}, u32[]{:S(2)}) %all-to-all-start.5) | async-done | bytes 2457632 | tf_op jit(solution)/shard_map/all_to_all | solution.py:75
  441.6 4.6 copy.355
  452.7 5.5 reshape.600
  458.2 4.1 multiply_reduce_fusion.6
  464.0 5.9 convert_reduce_fusion.1
  482.5 4.2 all-to-all-start.6
  486.7 5.1 convolution_bitcast_fusion
  494.9 3.9 all-to-all-done.6
  502.2 23.0 %while.47 = (s32[]{:T(128)}, bf16[4,4,200,3,2,64]{2,5,4,3,1,0:T(8,128)(2,1)}, bf16[4,4,200,3,2,64]{2,5,4,1,3,0:T(8,128)(2,1)}, s32[4,4]{1,0:T(4,128)S(1)}, f32[4...) while((s32[]{:T(128)}, bf16[4,4,200,3,2,64]{2,5,4,3,1,0:T(8,128)(2,1)}, ...), condition=%wide.region_27.28_spmd, body=%wide.region_25.27_spmd.sunk | while | flops 208805600 | bytes 15790513 | solution.py:129
  525.3 4.6 copy.363
  529.9 4.6 all-to-all-start.7
  534.6 5.0 convolution_bitcast_fusion.4
  548.2 16.0 %all-to-all-done.7 = bf16[16,200,3,1,128]{4,1,3,2,0:T(8,128)(2,1)} async-done(((bf16[16,200,3,1,128]{4,1,3,2,0:T(8,128)(2,1)}), bf16[16,200,3,1,128]{4,1,3,2,0:T(8,128)(2,1)}, u32[]{:S(2)}, u32[]{:S(2)}) %all-to-all-start.7) | async-done | bytes 2457632 | tf_op jit(solution)/shard_map/all_to_all | solution.py:75
  564.1 4.7 copy.364
  575.3 4.5 reshape.604
  600.1 4.5 fusion.77
  607.9 41.2 %all-reduce = (f32[2,2,384]{2,1,0:T(2,128)S(1)}, f32[2,3840]{1,0:T(2,128)S(1)}) all-reduce(f32[2,2,384]{2,1,0:T(2,128)S(1)} %pad_maximum_fusion.26, f32[2,3840]{1,0:T(2,128)S(1)} %pad_maximum_fusion.22), channel_id=1, replica_groups=mesh['dp'=8,'tok'=4] {'dp','tok'}, use_global_device_ids=true, to_apply=%region_42.43 | all-reduce | flops 9216 | bytes 73728 | tf_op jit(solution)/shard_map/psum | solution.py:307
  653.2 179.8 %all-reduce.4.cloned.1.call-done = (f32[2,384,1152]{2,1,0:T(8,128)}, f32[2,384,384]{2,1,0:T(8,128)}, f32[2,384,1536]{2,1,0:T(8,128)}, f32[2,1536,384]{2,1,0:T(8,128)}) async-done(((f32[2,384,1152]{2,1,0:T(8,128)}, f32[2,384,384]{2,1,0:T(8,128)}, f32[2,384,1536]{2,1,0:T(8,128)}, f32[2,1536,384]{2,1,0:T(8,128)}), (f32[2,384,1152]{2,1,0:T(8,128)}, f32[2,384,384]{2,1,0:T(8,128)}, f32[2,384,1536]{2,1,0:T(8,128)}, ...) | async-done | bytes 14155792 | tf_op jit(solution)/shard_map/psum | solution.py:307
  835.3 3.5 multiply_reduce_fusion.4
  853.7 3.6 subtract_bitcast_fusion
  877.9 12.1 %concatenate.67 = f32[443520]{0:T(1024)} concatenate(f32[110592]{0:T(1024)S(1)} %copy-done.47, f32[36864]{0:T(1024)S(1)} %copy-done.54, f32[147456]{0:T(1024)S(1)} %copy-done.42, f32[147456]{0:T(1024)S(1)} %copy-done.41, f32[192]{0:T(256)S(1)} %copy-done.92, f32[960]{0:T(1024)S(1)} %reshape.611), dimensions={0} | concatenate | bytes 3548160 | tf_op jit(solution)/shard_map/concatenate | solution.py:329
  (578 shorter events, 258.9 us)
Async XLA Ops:
  7.2 65.6 %copy-start.1 = (bf16[4,200,384]{2,1,0:T(8,128)(2,1)S(1)}, bf16[4,200,384]{2,1,0:T(8,128)(2,1)}, u32[]{:S(2)}) copy-start(bf16[4,200,384]{2,1,0:T(8,128)(2,1)} %param.23) | copy-start | bytes 1843204
  7.2 71.7 %all-gather.5.cloned.1.call-start = ((), (), s32[]{:S(2)}) async-start(), calls=%async_computation.8 | async-start | bytes 1990656 | tf_op jit(solution)/shard_map/all_gather | solution.py:168
  69.6 9.2 %copy-start.64 = (f32[1,3840]{1,0:T(1,128)}, f32[1,3840]{1,0:T(1,128)S(1)}, u32[]{:S(2)}) copy-start(f32[1,3840]{1,0:T(1,128)S(1)} %get-tuple-element.470) | copy-start | bytes 46084
  72.8 6.1 copy-start.62
  97.2 5.5 copy-start.107
  97.2 34.3 %all-to-all-start = ((bf16[4,200,3,4,128]{4,1,2,0,3:T(8,128)(2,1)}), bf16[4,200,3,4,128]{4,1,2,0,3:T(8,128)(2,1)}, u32[]{:S(2)}, u32[]{:S(2)}) async-start(bf16[4,200,3,4,128]{4,1,2,0,3:T(8,128)(2,1)} %copy.334), calls=%async_computation | async-start | bytes 4915200 | tf_op jit(solution)/shard_map/all_to_all | solution.py:54
  101.9 96.3 %all-gather.7.cloned.1.call-start = ((), (), s32[]{:S(2)}) async-start(), calls=%async_computation.9 | async-start | bytes 2654208 | tf_op jit(solution)/shard_map/all_gather | solution.py:170
  149.6 9.0 %copy-start = (bf16[4,4,200,3,2,64]{2,5,4,1,3,0:T(8,128)(2,1)}, bf16[4,4,200,3,2,64]{2,5,4,1,3,0:T(8,128)(2,1)S(1)}, u32[]{:S(2)}) copy-start(bf16[4,4,200,3,2,64]{2,5,4,1,3,0:T(8,128)(2,1)S(1)} %get-tuple-element.738) | copy-start | bytes 7372804
  152.5 41.4 %all-to-all-start.1 = ((bf16[16,200,1,128]{3,1,2,0:T(8,128)(2,1)}), bf16[16,200,1,128]{3,1,2,0:T(8,128)(2,1)}, u32[]{:S(2)}, u32[]{:S(2)}) async-start(bf16[16,200,1,128]{3,1,2,0:T(8,128)(2,1)} %copy.337), calls=%async_computation.1 | async-start | bytes 1638400 | tf_op jit(solution)/shard_map/all_to_all | solution.py:61
  156.7 58.0 %all-gather.9.cloned.1.call-start = ((), (), s32[]{:S(2)}) async-start(), calls=%async_computation.10 | async-start | bytes 2654208 | tf_op jit(solution)/shard_map/all_gather | solution.py:171
  160.9 37.4 %copy-start.83 = (f32[1536]{0:T(1024)}, f32[1536]{0:T(1024)S(1)}, u32[]{:S(2)}) copy-start(f32[1536]{0:T(1024)S(1)} %get-tuple-element.494) | copy-start | bytes 18436
  197.8 16.9 %copy-start.4 = (f32[800,384]{1,0:T(8,128)}, f32[800,384]{1,0:T(8,128)S(1)}, u32[]{:S(2)}) copy-start(f32[800,384]{1,0:T(8,128)S(1)} %get-tuple-element.476) | copy-start | bytes 3686404
  197.8 15.0 %copy-start.58 = (f32[800]{0:T(1024)}, f32[800]{0:T(1024)S(1)}, u32[]{:S(2)}) copy-start(f32[800]{0:T(1024)S(1)} %broadcast_multiply_fusion.10) | copy-start | bytes 9604
  198.2 14.7 %copy-start.60 = (f32[800]{0:T(1024)}, f32[800]{0:T(1024)S(1)}, u32[]{:S(2)}) copy-start(f32[800]{0:T(1024)S(1)} %add_rsqrt_fusion.2) | copy-start | bytes 9604
  198.3 16.4 %copy-start.106 = (f32[384]{0:T(512)S(1)}, f32[384]{0:T(512)}, u32[]{:S(2)}) copy-start(f32[384]{0:T(512)} %get-tuple-element.370) | copy-start | bytes 4612
  246.6 34.2 %all-to-all-start.2 = ((bf16[4,200,3,4,128]{4,1,2,0,3:T(8,128)(2,1)}), bf16[4,200,3,4,128]{4,1,2,0,3:T(8,128)(2,1)}, u32[]{:S(2)}, u32[]{:S(2)}) async-start(bf16[4,200,3,4,128]{4,1,2,0,3:T(8,128)(2,1)} %copy.342), calls=%async_computation.2 | async-start | bytes 4915200 | tf_op jit(solution)/shard_map/all_to_all | solution.py:54
  251.2 33.8 %copy-start.96 = (s32[4,4]{1,0:T(4,128)S(1)}, s32[4,4]{1,0:T(4,128)}, u32[]{:S(2)}) copy-start(s32[4,4]{1,0:T(4,128)} %get-tuple-element.772) | copy-start | bytes 196
  293.3 6.5 copy-start.108
  295.5 16.3 %all-to-all-start.3 = ((bf16[16,200,1,128]{3,1,2,0:T(8,128)(2,1)}), bf16[16,200,1,128]{3,1,2,0:T(8,128)(2,1)}, u32[]{:S(2)}, u32[]{:S(2)}) async-start(bf16[16,200,1,128]{3,1,2,0:T(8,128)(2,1)} %copy.345), calls=%async_computation.3 | async-start | bytes 1638400 | tf_op jit(solution)/shard_map/all_to_all | solution.py:61
  300.0 15.2 %copy-start.93 = (pred[800]{0:T(1024)(128)(4,1)}, pred[800]{0:T(1024)(128)(4,1)S(1)}, u32[]{:S(2)}) copy-start(pred[800]{0:T(1024)(128)(4,1)S(1)} %lt.134) | copy-start | bytes 2404
  323.0 19.7 %copy-start.6 = (f32[800,384]{1,0:T(8,128)}, f32[800,384]{1,0:T(8,128)S(1)}, u32[]{:S(2)}) copy-start(f32[800,384]{1,0:T(8,128)S(1)} %get-tuple-element.482) | copy-start | bytes 3686404
  323.4 12.8 %copy-start.53 = (bf16[4,200,384]{2,1,0:T(8,128)(2,1)S(1)}, bf16[4,200,384]{2,1,0:T(8,128)(2,1)}, u32[]{:S(2)}) copy-start(bf16[4,200,384]{2,1,0:T(8,128)(2,1)} %get-tuple-element.444) | copy-start | bytes 1843204
  323.4 12.8 %copy-start.109 = (bf16[2,1536,384]{2,1,0:T(8,128)(2,1)S(1)}, bf16[2,1536,384]{2,1,0:T(8,128)(2,1)}, u32[]{:S(2)}) copy-start(bf16[2,1536,384]{2,1,0:T(8,128)(2,1)} %all-gather.9.cloned.1.call-done) | copy-start | bytes 7077892
  358.5 16.3 %all-to-all-start.4 = ((bf16[4,200,4,128]{3,1,0,2:T(8,128)(2,1)}), bf16[4,200,4,128]{3,1,0,2:T(8,128)(2,1)}, u32[]{:S(2)}, u32[]{:S(2)}) async-start(bf16[4,200,4,128]{3,1,0,2:T(8,128)(2,1)} %copy.350), calls=%async_computation.4 | async-start | bytes 1638400 | tf_op jit(solution)/shard_map/all_to_all | solution.py:68
  407.2 34.3 %all-to-all-start.5 = ((bf16[16,200,3,1,128]{4,1,3,2,0:T(8,128)(2,1)}), bf16[16,200,3,1,128]{4,1,3,2,0:T(8,128)(2,1)}, u32[]{:S(2)}, u32[]{:S(2)}) async-start(bf16[16,200,3,1,128]{4,1,3,2,0:T(8,128)(2,1)} %copy.354), calls=%async_computation.5 | async-start | bytes 4915200 | tf_op jit(solution)/shard_map/all_to_all | solution.py:75
  452.7 5.5 copy-start.15
  463.5 8.6 copy-start.28
  464.0 5.9 copy-start.5
  464.0 5.9 copy-start.59
  464.0 5.9 copy-start.61
  464.0 5.9 copy-start.67
  464.0 5.9 copy-start.112
  482.5 16.3 %all-to-all-start.6 = ((bf16[4,200,4,128]{3,1,0,2:T(8,128)(2,1)}), bf16[4,200,4,128]{3,1,0,2:T(8,128)(2,1)}, u32[]{:S(2)}, u32[]{:S(2)}) async-start(bf16[4,200,4,128]{3,1,0,2:T(8,128)(2,1)} %copy.359), calls=%async_computation.6 | async-start | bytes 1638400 | tf_op jit(solution)/shard_map/all_to_all | solution.py:68
  486.7 5.1 copy-start.13
  486.7 5.1 copy-start.20
  529.9 34.3 %all-to-all-start.7 = ((bf16[16,200,3,1,128]{4,1,3,2,0:T(8,128)(2,1)}), bf16[16,200,3,1,128]{4,1,3,2,0:T(8,128)(2,1)}, u32[]{:S(2)}, u32[]{:S(2)}) async-start(bf16[16,200,3,1,128]{4,1,3,2,0:T(8,128)(2,1)} %copy.363), calls=%async_computation.7 | async-start | bytes 4915200 | tf_op jit(solution)/shard_map/all_to_all | solution.py:75
  534.5 298.5 %all-reduce.4.cloned.1.call-start = ((), (), s32[]{:S(2)}) async-start(), calls=%async_computation.11 | async-start | bytes 28311552 | tf_op jit(solution)/shard_map/psum | solution.py:307
  534.6 5.0 copy-start.29
  534.6 5.0 copy-start.115
  600.0 5.0 copy-start.24
  607.4 43.0 %copy-start.10 = (f32[800,384]{1,0:T(8,128)S(1)}, f32[800,384]{1,0:T(8,128)}, u32[]{:S(2)}) copy-start(f32[800,384]{1,0:T(8,128)} %copy-done.8) | copy-start | bytes 3686404
  833.0 5.8 copy-start.17
  841.2 5.7 copy-start.75
  841.2 5.7 copy-start.91
  841.2 5.9 copy-start.86
  841.2 5.9 copy-start.95
  848.4 5.3 copy-start.31
  848.4 5.3 copy-start.32
  (81 other events, 238.9 us)
Sparse Core Ops, SparseCore 0:
  10.9 50.0 all-gather.4
  105.5 51.8 all-gather.6
  160.3 54.3 all-gather.8
  585.1 247.8 all-reduce.3
where the time goes:
time: 911 us; the launch traced here: 898 us
  waiting for transfers between devices  305 us (33%)
  local copies, waits for them, and re-layouts  189 us (21%)
  blocking collectives  133 us (15%)
  matrix products  127 us (14%)
  other arithmetic  86.8 us (10%)
  starting transfers between devices  35.5 us (4%)
  between operations  20.9 us (2%)
    psum x1, waiting for transfers between devices, on_device(): lax.psum((grad_qkv_all, grad_proj_all, grad_fc1_all, grad_fc2_all, grad_g...  180 us
    all_to_all x2, waiting for transfers between devices, qkv_to_heads(): lax.all_to_all(sending, 'tok', split_axis=3, concat_axis=0, tiled=True)  57.7 us
    psum x1, blocking collectives, on_device(): lax.psum((grad_qkv_all, grad_proj_all, grad_fc1_all, grad_fc2_all, grad_g...  41.2 us
    all_to_all x2, waiting for transfers between devices, grads_to_rows(): lax.all_to_all(sending, 'tok', split_axis=0, concat_axis=3, tiled=True)  40.9 us
    all_gather x1, blocking collectives, on_device(): lax.all_gather(w_proj.astype(jnp.bfloat16), 'dp', axis=2, tiled=True)  33.1 us
    all_gather x1, blocking collectives, on_device(): lax.all_gather(norm_gains.astype(jnp.bfloat16), 'dp', axis=2, tiled=True)  31.1 us
    all_gather x1, blocking collectives, on_device(): lax.all_gather(biases.astype(jnp.bfloat16), 'dp', axis=1, tiled=True)  27.9 us
    dot_general x2, matrix products, on_device(): jnp.dot(a_second, up_weight, preferred_element_type=jnp.float32)  27.4 us
  transfers between devices with their start and end apart: 12, of which 9 were waited for; matrix products, arithmetic and copies ran while one was open for 12% of the time, Pallas kernels for 0%

commit v1 on v0

--- a/solution.py
+++ b/solution.py
@@ -304,9 +304,12 @@
     masters = (w_qkv, w_proj, w_fc1, w_fc2, norm_gains, biases)
     shard_dims = (2, 2, 2, 1, 2, 1)
     dp_index = lax.axis_index("dp")
-    summed = lax.psum(
-        (grad_qkv_all, grad_proj_all, grad_fc1_all, grad_fc2_all, grad_gain_all, grad_bias_all),
-        ("dp", "tok"),
+    summed = jax.lax.psum(
+        jax.lax.psum(
+            (grad_qkv_all, grad_proj_all, grad_fc1_all, grad_fc2_all, grad_gain_all, grad_bias_all),
+            "tok",
+        ),
+        axis_name="dp",
     )
     squares = sum_squares(summed)
     shares = tuple(

time: 911 us -> 1360 us (1.49)
  waiting for transfers between devices: 305 us -> 736 us
    psum x1 -> x2, waiting for transfers between devices: 180 us -> 612 us  [the longest x1 367 us: on_device(): jax.lax.psum(jax.lax.psum((grad_qkv_all, grad_proj_all, grad_fc1_all, gra...]
    psum x1 -> x2, blocking collectives: 41.2 us -> 52.4 us  [the longest x1 40.9 us: on_device(): jax.lax.psum(jax.lax.psum((grad_qkv_all, grad_proj_all, grad_fc1_all, gra...]
  transfers between devices with their start and end apart: 12 -> 13, of which waited for: 9 -> 9; matrix products, arithmetic and copies ran while one was open for 12% -> 8% of each run, Pallas kernels for 0% -> 0%
where the time goes in v1:
time: 1360 us; the launch traced here: 1340 us
  waiting for transfers between devices  736 us (54%)
  local copies, waits for them, and re-layouts  182 us (13%)
  blocking collectives  144 us (11%)
  matrix products  127 us (9%)
  other arithmetic  96.7 us (7%)
  starting transfers between devices  36 us (3%)
  between operations  21 us (2%)
    psum x1, waiting for transfers between devices, on_device(): jax.lax.psum(jax.lax.psum((grad_qkv_all, grad_proj_all, grad_fc1_all, gra...  367 us
    psum x1, waiting for transfers between devices, on_device(): jax.lax.psum((grad_qkv_all, grad_proj_all, grad_fc1_all, grad_fc2_all, gr...  245 us
    all_to_all x2, waiting for transfers between devices, qkv_to_heads(): lax.all_to_all(sending, 'tok', split_axis=3, concat_axis=0, tiled=True)  57.7 us
    psum x1, blocking collectives, on_device(): jax.lax.psum(jax.lax.psum((grad_qkv_all, grad_proj_all, grad_fc1_all, gra...  40.9 us
    all_to_all x2, waiting for transfers between devices, grads_to_rows(): lax.all_to_all(sending, 'tok', split_axis=0, concat_axis=3, tiled=True)  40.6 us
    all_gather x1, blocking collectives, on_device(): lax.all_gather(w_proj.astype(jnp.bfloat16), 'dp', axis=2, tiled=True)  33.1 us
    all_gather x1, blocking collectives, on_device(): lax.all_gather(norm_gains.astype(jnp.bfloat16), 'dp', axis=2, tiled=True)  31.1 us
    all_gather x1, blocking collectives, on_device(): lax.all_gather(biases.astype(jnp.bfloat16), 'dp', axis=1, tiled=True)  27.9 us
  transfers between devices with their start and end apart: 13, of which 9 were waited for; matrix products, arithmetic and copies ran while one was open for 8% of the time, Pallas kernels for 0%

profile of v1, /device:TPU:0, one launch (start us, length us, event | category | flops | bytes accessed | tf_op | source)
XLA Modules:
  0.0 1342.6 jit_solution(11258011042699468094)
XLA Ops:
  9.7 27.9 %all-gather = bf16[8,480,2]{1,2,0:T(2,128)(2,1)S(1)} all-gather(bf16[1,480,2]{1,2,0:T(2,128)(2,1)S(1)} %convert_bitcast_fusion), channel_id=1, replica_groups=mesh['dp'=8,'tok'=4] {'dp'}, dimensions={0}, use_global_device_ids=true | all-gather | bytes 17280 | tf_op jit(solution)/shard_map/all_gather | solution.py:173
  38.5 31.1 %all_gather.18 = bf16[2,2,384]{1,0,2:T(2,128)(2,1)S(1)} all-gather(bf16[2,2,48]{1,0,2:T(2,128)(2,1)S(1)} %copy.330), channel_id=1, replica_groups=mesh['dp'=8,'tok'=4] {'dp'}, dimensions={2}, use_global_device_ids=true | all-gather | bytes 3456 | tf_op jit(solution)/shard_map/all_gather | solution.py:172
  73.5 4.9 slice_reduce_fusion
  83.9 5.7 reshape.586
  97.2 4.6 all-to-all-start
  103.4 28.1 %all-to-all-done = bf16[4,200,3,4,128]{4,1,2,0,3:T(8,128)(2,1)} async-done(((bf16[4,200,3,4,128]{4,1,2,0,3:T(8,128)(2,1)}), bf16[4,200,3,4,128]{4,1,2,0,3:T(8,128)(2,1)}, u32[]{:S(2)}, u32[]{:S(2)}) %all-to-all-start) | async-done | bytes 2457632 | tf_op jit(solution)/shard_map/all_to_all | solution.py:54
  136.3 13.3 while.44
  152.5 4.2 all-to-all-start.1
  160.9 33.1 %all_gather.21 = bf16[2,384,384]{1,2,0:T(8,128)(2,1)S(1)} all-gather(bf16[2,384,48]{1,2,0:T(8,128)(2,1)S(1)} %convert_element_type.200), channel_id=1, replica_groups=mesh['dp'=8,'tok'=4] {'dp'}, dimensions={2}, use_global_device_ids=true | all-gather | bytes 663552 | tf_op jit(solution)/shard_map/all_gather | solution.py:169
  200.6 14.6 %fusion.38 = (bf16[800,1536]{1,0:T(8,128)(2,1)}, f32[800,1536]{1,0:T(8,128)}) fusion(f32[1536]{0:T(1024)S(1)} %get-tuple-element.500, bf16[2,384,1536]{1,2,0:T(8,128)(2,1)} %all-gather.7.cloned.1.call-done, f32[800,384]{1,0:T(8,128)S(1)} %get-tuple-element.482, f32[384]{0:T(512)S(1)} %copy-done.72, f32[384]{0:T(512)S(1)} %copy-done.68, ...), kind=kOutput, calls=%fused_computation.94 | convolution fusion | flops 1026355200 | bytes 9796864 | tf_op jit(solution)/shard_map/dot_general | solution.py:209
  215.3 3.7 fusion.121
  223.8 5.7 reshape.591
  230.5 13.7 %pad_maximum_fusion.4 = bf16[4,200,3,8,64]{1,0,4,3,2:T(4,128)(2,1)S(1)} fusion(bf16[4,200,3,1,64]{1,0,4,3,2:T(4,128)(2,1)S(1)} %broadcast.401, bf16[4,200,3,1,64]{1,0,4,3,2:T(4,128)(2,1)S(1)} %slice.397, bf16[4,200,3,5,64]{1,0,4,3,2:T(4,128)(2,1)S(1)} %slice.396), kind=kLoop, calls=%fused_computation.148 | loop fusion | flops 3686400 | bytes 4608000 | tf_op jit(solution)/shard_map/concatenate | solution.py:42
  244.2 3.7 copy.342
  247.8 4.6 all-to-all-start.2
  252.4 29.6 %all-to-all-done.2 = bf16[4,200,3,4,128]{4,1,2,0,3:T(8,128)(2,1)} async-done(((bf16[4,200,3,4,128]{4,1,2,0,3:T(8,128)(2,1)}), bf16[4,200,3,4,128]{4,1,2,0,3:T(8,128)(2,1)}, u32[]{:S(2)}, u32[]{:S(2)}) %all-to-all-start.2) | async-done | bytes 2457632 | tf_op jit(solution)/shard_map/all_to_all | solution.py:54
  286.2 8.3 while.45
  296.7 4.2 all-to-all-start.3
  303.9 9.1 all-to-all-done.3
  324.6 12.8 fusion.41
  337.3 4.3 convert_reduce_fusion
  359.1 4.2 all-to-all-start.4
  363.3 12.1 all-to-all-done.4
  379.7 23.5 %while.46 = (s32[]{:T(128)}, bf16[4,4,200,3,2,64]{2,5,4,3,1,0:T(8,128)(2,1)}, bf16[4,4,200,3,2,64]{2,5,4,1,3,0:T(8,128)(2,1)S(1)}, s32[4,4]{1,0:T(4,128)S(1)}, f...) while((s32[]{:T(128)}, bf16[4,4,200,3,2,64]{2,5,4,3,1,0:T(8,128)(2,1)}, ...), condition=%wide.region_20.21_spmd, body=%wide.region_18.20_spmd.sunk | while | flops 208805600 | bytes 15433129 | solution.py:129
  403.2 4.6 copy.354
  407.8 4.7 all-to-all-start.5
  412.5 4.7 convolution_bitcast_fusion.2
  417.2 24.9 %all-to-all-done.5 = bf16[16,200,3,1,128]{4,1,3,2,0:T(8,128)(2,1)} async-done(((bf16[16,200,3,1,128]{4,1,3,2,0:T(8,128)(2,1)}), bf16[16,200,3,1,128]{4,1,3,2,0:T(8,128)(2,1)}, u32[]{:S(2)}, u32[]{:S(2)}) %all-to-all-start.5) | async-done | bytes 2457632 | tf_op jit(solution)/shard_map/all_to_all | solution.py:75
  442.1 4.6 copy.355
  453.3 5.5 reshape.600
  458.8 4.1 multiply_reduce_fusion.6
  464.6 5.9 convert_reduce_fusion.1
  483.0 4.2 all-to-all-start.6
  487.2 5.1 convolution_bitcast_fusion
  495.4 3.9 all-to-all-done.6
  502.8 23.0 %while.47 = (s32[]{:T(128)}, bf16[4,4,200,3,2,64]{2,5,4,3,1,0:T(8,128)(2,1)}, bf16[4,4,200,3,2,64]{2,5,4,1,3,0:T(8,128)(2,1)}, s32[4,4]{1,0:T(4,128)S(1)}, f32[4...) while((s32[]{:T(128)}, bf16[4,4,200,3,2,64]{2,5,4,3,1,0:T(8,128)(2,1)}, ...), condition=%wide.region_27.28_spmd, body=%wide.region_25.27_spmd.sunk | while | flops 208805600 | bytes 15790513 | solution.py:129
  525.7 4.6 copy.363
  530.3 4.6 all-to-all-start.7
  535.3 5.0 convolution_bitcast_fusion.4
  548.8 15.7 %all-to-all-done.7 = bf16[16,200,3,1,128]{4,1,3,2,0:T(8,128)(2,1)} async-done(((bf16[16,200,3,1,128]{4,1,3,2,0:T(8,128)(2,1)}), bf16[16,200,3,1,128]{4,1,3,2,0:T(8,128)(2,1)}, u32[]{:S(2)}, u32[]{:S(2)}) %all-to-all-start.7) | async-done | bytes 2457632 | tf_op jit(solution)/shard_map/all_to_all | solution.py:75
  564.6 4.5 copy.364
  575.6 5.5 reshape.604
  586.4 245.1 %all-reduce.9.cloned.1.call-done = (f32[2,384,1152]{2,1,0:T(8,128)}, f32[2,384,384]{2,1,0:T(8,128)}, f32[2,384,1536]{2,1,0:T(8,128)}, f32[2,1536,384]{2,1,0:T(8,128)}) async-done(((f32[2,384,1152]{2,1,0:T(8,128)}, f32[2,384,384]{2,1,0:T(8,128)}, f32[2,384,1536]{2,1,0:T(8,128)}, f32[2,1536,384]{2,1,0:T(8,128)}), (f32[2,384,1152]{2,1,0:T(8,128)}, f32[2,384,384]{2,1,0:T(8,128)}, f32[2,384,1536]{2,1,0:T(8,128)}, ...) | async-done | bytes 14155792 | tf_op jit(solution)/shard_map/psum | solution.py:308
  846.3 4.4 fusion.77
  854.2 11.5 all-reduce.2
  865.7 40.9 %all-reduce = (f32[2,2,384]{2,1,0:T(2,128)S(1)}, f32[2,3840]{1,0:T(2,128)S(1)}) all-reduce(f32[2,2,384]{2,1,0:T(2,128)S(1)} %get-tuple-element.426, f32[2,3840]{1,0:T(2,128)S(1)} %get-tuple-element.427), channel_id=1, replica_groups=mesh['dp'=8,'tok'=4] {'dp'}, use_global_device_ids=true, to_apply=%region_47.48 | all-reduce | flops 9216 | bytes 73728 | tf_op jit(solution)/shard_map/psum | solution.py:307
  910.7 366.9 %all-reduce.7.cloned.1.call-done = (f32[2,384,1152]{2,1,0:T(8,128)}, f32[2,384,384]{2,1,0:T(8,128)}, f32[2,384,1536]{2,1,0:T(8,128)}, f32[2,1536,384]{2,1,0:T(8,128)}) async-done(((f32[2,384,1152]{2,1,0:T(8,128)}, f32[2,384,384]{2,1,0:T(8,128)}, f32[2,384,1536]{2,1,0:T(8,128)}, f32[2,1536,384]{2,1,0:T(8,128)}), (f32[2,384,1152]{2,1,0:T(8,128)}, f32[2,384,384]{2,1,0:T(8,128)}, f32[2,384,1536]{2,1,0:T(8,128)}, ...) | async-done | bytes 14155792 | tf_op jit(solution)/shard_map/psum | solution.py:307
  1322.4 12.1 concatenate.67
  (586 shorter events, 266.6 us)
Async XLA Ops:
  7.2 65.6 %copy-start.1 = (bf16[4,200,384]{2,1,0:T(8,128)(2,1)S(1)}, bf16[4,200,384]{2,1,0:T(8,128)(2,1)}, u32[]{:S(2)}) copy-start(bf16[4,200,384]{2,1,0:T(8,128)(2,1)} %param.23) | copy-start | bytes 1843204
  7.2 71.7 %all-gather.5.cloned.1.call-start = ((), (), s32[]{:S(2)}) async-start(), calls=%async_computation.8 | async-start | bytes 1990656 | tf_op jit(solution)/shard_map/all_gather | solution.py:168
  69.6 9.2 copy-start.66
  72.8 6.1 copy-start.64
  97.2 5.5 copy-start.109
  97.2 34.3 %all-to-all-start = ((bf16[4,200,3,4,128]{4,1,2,0,3:T(8,128)(2,1)}), bf16[4,200,3,4,128]{4,1,2,0,3:T(8,128)(2,1)}, u32[]{:S(2)}, u32[]{:S(2)}) async-start(bf16[4,200,3,4,128]{4,1,2,0,3:T(8,128)(2,1)} %copy.334), calls=%async_computation | async-start | bytes 4915200 | tf_op jit(solution)/shard_map/all_to_all | solution.py:54
  101.9 98.7 %all-gather.7.cloned.1.call-start = ((), (), s32[]{:S(2)}) async-start(), calls=%async_computation.9 | async-start | bytes 2654208 | tf_op jit(solution)/shard_map/all_gather | solution.py:170
  149.6 9.0 copy-start
  152.5 41.4 %all-to-all-start.1 = ((bf16[16,200,1,128]{3,1,2,0:T(8,128)(2,1)}), bf16[16,200,1,128]{3,1,2,0:T(8,128)(2,1)}, u32[]{:S(2)}, u32[]{:S(2)}) async-start(bf16[16,200,1,128]{3,1,2,0:T(8,128)(2,1)} %copy.337), calls=%async_computation.1 | async-start | bytes 1638400 | tf_op jit(solution)/shard_map/all_to_all | solution.py:61
  156.7 58.5 %all-gather.9.cloned.1.call-start = ((), (), s32[]{:S(2)}) async-start(), calls=%async_computation.10 | async-start | bytes 2654208 | tf_op jit(solution)/shard_map/all_gather | solution.py:171
  160.9 39.7 %copy-start.85 = (f32[1536]{0:T(1024)}, f32[1536]{0:T(1024)S(1)}, u32[]{:S(2)}) copy-start(f32[1536]{0:T(1024)S(1)} %get-tuple-element.500) | copy-start | bytes 18436
  193.9 5.5 copy-start.24
  200.2 15.1 %copy-start.4 = (f32[800,384]{1,0:T(8,128)}, f32[800,384]{1,0:T(8,128)S(1)}, u32[]{:S(2)}) copy-start(f32[800,384]{1,0:T(8,128)S(1)} %get-tuple-element.482) | copy-start | bytes 3686404
  200.2 15.0 %copy-start.60 = (f32[800]{0:T(1024)}, f32[800]{0:T(1024)S(1)}, u32[]{:S(2)}) copy-start(f32[800]{0:T(1024)S(1)} %broadcast_multiply_fusion.10) | copy-start | bytes 9604
  200.5 14.7 %copy-start.62 = (f32[800]{0:T(1024)}, f32[800]{0:T(1024)S(1)}, u32[]{:S(2)}) copy-start(f32[800]{0:T(1024)S(1)} %add_rsqrt_fusion.2) | copy-start | bytes 9604
  200.6 14.6 %copy-start.108 = (f32[384]{0:T(512)S(1)}, f32[384]{0:T(512)}, u32[]{:S(2)}) copy-start(f32[384]{0:T(512)} %get-tuple-element.370) | copy-start | bytes 4612
  247.8 34.2 %all-to-all-start.2 = ((bf16[4,200,3,4,128]{4,1,2,0,3:T(8,128)(2,1)}), bf16[4,200,3,4,128]{4,1,2,0,3:T(8,128)(2,1)}, u32[]{:S(2)}, u32[]{:S(2)}) async-start(bf16[4,200,3,4,128]{4,1,2,0,3:T(8,128)(2,1)} %copy.342), calls=%async_computation.2 | async-start | bytes 4915200 | tf_op jit(solution)/shard_map/all_to_all | solution.py:54
  252.4 33.8 %copy-start.98 = (s32[4,4]{1,0:T(4,128)S(1)}, s32[4,4]{1,0:T(4,128)}, u32[]{:S(2)}) copy-start(s32[4,4]{1,0:T(4,128)} %get-tuple-element.796) | copy-start | bytes 196
  294.5 6.5 copy-start.110
  296.7 16.3 %all-to-all-start.3 = ((bf16[16,200,1,128]{3,1,2,0:T(8,128)(2,1)}), bf16[16,200,1,128]{3,1,2,0:T(8,128)(2,1)}, u32[]{:S(2)}, u32[]{:S(2)}) async-start(bf16[16,200,1,128]{3,1,2,0:T(8,128)(2,1)} %copy.345), calls=%async_computation.3 | async-start | bytes 1638400 | tf_op jit(solution)/shard_map/all_to_all | solution.py:61
  301.2 15.2 %copy-start.95 = (pred[800]{0:T(1024)(128)(4,1)}, pred[800]{0:T(1024)(128)(4,1)S(1)}, u32[]{:S(2)}) copy-start(pred[800]{0:T(1024)(128)(4,1)S(1)} %lt.134) | copy-start | bytes 2404
  324.1 19.7 %copy-start.6 = (f32[800,384]{1,0:T(8,128)}, f32[800,384]{1,0:T(8,128)S(1)}, u32[]{:S(2)}) copy-start(f32[800,384]{1,0:T(8,128)S(1)} %get-tuple-element.488) | copy-start | bytes 3686404
  324.5 12.8 copy-start.54
  324.6 12.8 copy-start.111
  359.1 16.3 %all-to-all-start.4 = ((bf16[4,200,4,128]{3,1,0,2:T(8,128)(2,1)}), bf16[4,200,4,128]{3,1,0,2:T(8,128)(2,1)}, u32[]{:S(2)}, u32[]{:S(2)}) async-start(bf16[4,200,4,128]{3,1,0,2:T(8,128)(2,1)} %copy.350), calls=%async_computation.4 | async-start | bytes 1638400 | tf_op jit(solution)/shard_map/all_to_all | solution.py:68
  407.8 34.3 %all-to-all-start.5 = ((bf16[16,200,3,1,128]{4,1,3,2,0:T(8,128)(2,1)}), bf16[16,200,3,1,128]{4,1,3,2,0:T(8,128)(2,1)}, u32[]{:S(2)}, u32[]{:S(2)}) async-start(bf16[16,200,3,1,128]{4,1,3,2,0:T(8,128)(2,1)} %copy.354), calls=%async_computation.5 | async-start | bytes 4915200 | tf_op jit(solution)/shard_map/all_to_all | solution.py:75
  453.3 5.5 copy-start.15
  464.1 8.6 copy-start.27
  464.6 5.9 copy-start.5
  464.6 5.9 copy-start.61
  464.6 5.9 copy-start.63
  464.6 5.9 copy-start.69
  464.6 5.9 copy-start.114
  483.0 16.3 %all-to-all-start.6 = ((bf16[4,200,4,128]{3,1,0,2:T(8,128)(2,1)}), bf16[4,200,4,128]{3,1,0,2:T(8,128)(2,1)}, u32[]{:S(2)}, u32[]{:S(2)}) async-start(bf16[4,200,4,128]{3,1,0,2:T(8,128)(2,1)} %copy.359), calls=%async_computation.6 | async-start | bytes 1638400 | tf_op jit(solution)/shard_map/all_to_all | solution.py:68
  530.3 34.3 %all-to-all-start.7 = ((bf16[16,200,3,1,128]{4,1,3,2,0:T(8,128)(2,1)}), bf16[16,200,3,1,128]{4,1,3,2,0:T(8,128)(2,1)}, u32[]{:S(2)}, u32[]{:S(2)}) async-start(bf16[16,200,3,1,128]{4,1,3,2,0:T(8,128)(2,1)} %copy.363), calls=%async_computation.7 | async-start | bytes 4915200 | tf_op jit(solution)/shard_map/all_to_all | solution.py:75
  535.0 296.6 %all-reduce.9.cloned.1.call-start = ((), (), s32[]{:S(2)}) async-start(), calls=%async_computation.12 | async-start | bytes 28311552 | tf_op jit(solution)/shard_map/psum | solution.py:308
  575.6 5.5 copy-start.53
  586.1 691.4 %all-reduce.7.cloned.1.call-start = ((), (), s32[]{:S(2)}) async-start(), calls=%async_computation.11 | async-start | bytes 28311552 | tf_op jit(solution)/shard_map/psum | solution.py:307
  840.5 5.4 copy-start.3
  853.7 54.1 %copy-start.10 = (f32[800,384]{1,0:T(8,128)S(1)}, f32[800,384]{1,0:T(8,128)}, u32[]{:S(2)}) copy-start(f32[800,384]{1,0:T(8,128)} %copy-done.8) | copy-start | bytes 3686404
  1277.5 5.8 copy-start.17
  1285.7 5.7 copy-start.78
  1285.7 5.7 copy-start.93
  1285.7 5.9 copy-start.88
  1285.7 5.9 copy-start.97
  1292.9 5.4 copy-start.31
  1292.9 5.4 copy-start.32
  1292.9 5.4 copy-start.33
  (84 other events, 256.7 us)
Sparse Core Ops, SparseCore 0:
  10.9 50.0 all-gather.4
  105.5 51.8 all-gather.6
  160.3 54.3 all-gather.8
  586.2 245.2 all-reduce.8
  836.1 441.4 all-reduce.6
